TPU v7x, 32 devices: a whole 2x2x4 slice. The times are simulated.
32 devices in a mesh: seq: 8 (over z, core), fsdp: 4 (over y, x).
Axes of the slice: x: 2, y: 2, z: 4, core: 2. Of those that a mesh axis runs over, the one named last changes fastest.
Arguments:
- tokens: bfloat16 [4, 1024, 1024], P('fsdp', 'seq'), may hold values from -6 to 6
- ln1_gain: float32 [1024], replicated, may hold values from 0.25 to 1.75
- ln1_bias: float32 [1024], replicated, may hold values from -3 to 3
- qkv_weight: bfloat16 [1024, 3072], P(('seq', 'fsdp')), may hold values from -0.1875 to 0.1875
- qkv_bias: float32 [3072], replicated, may hold values from -2.5 to 2.5
- out_weight: bfloat16 [1024, 1024], P(('seq', 'fsdp')), may hold values from -3 to 3
- ln2_gain: float32 [1024], replicated, may hold values from 0.25 to 1.75
- ln2_bias: float32 [1024], replicated, may hold values from -3 to 3
- gate_up_weight: bfloat16 [1024, 5632], P(('seq', 'fsdp')), may hold values from -0.1875 to 0.1875
- down_weight: bfloat16 [2816, 1024], P(('seq', 'fsdp')), may hold values from -0.109375 to 0.109375
- out_grad: bfloat16 [4, 1024, 1024], P('fsdp', 'seq'), may hold values from -6 to 6
Outputs:
- block_out: bfloat16 [4, 1024, 1024], P('fsdp', 'seq')
- input_grad: float32 [4, 1024, 1024], P('fsdp', 'seq')
- ln1_gain_grad: float32 [1024], replicated
- ln1_bias_grad: float32 [1024], replicated
- qkv_weight_grad: float32 [1024, 3072], P(('seq', 'fsdp'))
- qkv_bias_grad: float32 [3072], replicated
- out_weight_grad: float32 [1024, 1024], P(('seq', 'fsdp'))
- ln2_gain_grad: float32 [1024], replicated
- ln2_bias_grad: float32 [1024], replicated
- gate_up_weight_grad: float32 [1024, 5632], P(('seq', 'fsdp'))
- down_weight_grad: float32 [2816, 1024], P(('seq', 'fsdp'))
All inputs are finite; a program needn't handle non-finite values.
Results may differ from a plain program's by a relative error of at most 0.011.
Values may be sent and summed in bfloat16 or wider, within the bound.
No kernel may reach another device: no remote copies, remote signals or barrier semaphores. Data moves between devices by JAX's collectives and lax.ppermute only.
A program may use at most 192 MiB of HBM per device.

v0:
```python
import jax
import jax.numpy as jnp
from jax import lax
from jax.sharding import PartitionSpec as P

H = 16
HD = 64
ROT = 16
EPS = 1e-05


def layer_norm(values, gain_vec, shift_vec):
    average = jnp.mean(values, axis=-1, keepdims=True)
    centred = values - average
    variance = jnp.mean(centred * centred, axis=-1, keepdims=True)
    return centred * lax.rsqrt(variance + EPS) * gain_vec + shift_vec


def rotary_tables(positions):
    half_rot = ROT // 2
    frequency = 10000.0 ** (-2.0 * jnp.arange(half_rot).astype(jnp.float32) / ROT)
    angles = positions.astype(jnp.float32)[:, None] * frequency[None, :]
    return (jnp.cos(angles)[:, None, :], jnp.sin(angles)[:, None, :])


def rotate(heads_in, positions):
    half_rot = ROT // 2
    cosines, sines = rotary_tables(positions)
    lower_half = heads_in[..., :half_rot]
    upper_half = heads_in[..., half_rot:ROT]
    return jnp.concatenate(
        [
            lower_half * cosines - upper_half * sines,
            upper_half * cosines + lower_half * sines,
            heads_in[..., ROT:],
        ],
        axis=-1,
    )


def unrotate(grads_in, positions):
    half_rot = ROT // 2
    cosines, sines = rotary_tables(positions)
    lower_half = grads_in[..., :half_rot]
    upper_half = grads_in[..., half_rot:ROT]
    return jnp.concatenate(
        [
            lower_half * cosines + upper_half * sines,
            upper_half * cosines - lower_half * sines,
            grads_in[..., ROT:],
        ],
        axis=-1,
    )


def swiglu(gate_up):
    half_width = gate_up.shape[-1] // 2
    return jax.nn.silu(gate_up[:, :half_width]) * gate_up[:, half_width:]


def contract_last(left, right):
    return lax.dot_general(
        left, right, (((1,), (1,)), ((), ())), preferred_element_type=jnp.float32
    )


def column_term(left, right):
    return lax.dot_general(
        left, right, (((0,), (0,)), ((), ())), preferred_element_type=jnp.float32
    )


def attend(queries, keys_in, values_in):
    length = queries.shape[0]
    block_rows = min(512, length)
    scaling = queries.shape[2] ** (-0.5)
    key_index = jnp.arange(length, dtype=jnp.int32)

    def one_block(args):
        query_block, first_row = args
        scores = (
            jnp.einsum("qhd,khd->hqk", query_block, keys_in, preferred_element_type=jnp.float32)
            * scaling
        )
        causal = (first_row + jnp.arange(block_rows, dtype=jnp.int32))[:, None] >= key_index[
            None, :
        ]
        scores = jnp.where(causal[None], scores, -jnp.inf)
        row_max = jnp.max(scores, axis=-1, keepdims=True)
        exponent = jnp.exp(scores - row_max)
        normaliser = jnp.sum(exponent, axis=-1, keepdims=True)
        weights = (exponent / normaliser).astype(jnp.bfloat16)
        out_block = jnp.einsum(
            "hqk,khd->qhd", weights, values_in, preferred_element_type=jnp.float32
        )
        return (out_block, (row_max + jnp.log(normaliser))[..., 0])

    blocks = queries.reshape(length // block_rows, block_rows, queries.shape[1], queries.shape[2])
    starts = jnp.arange(length // block_rows, dtype=jnp.int32) * block_rows
    out_blocks, totals = lax.map(one_block, (blocks, starts))
    return (out_blocks.reshape(queries.shape), totals)


def attend_back(queries, keys_in, values_in, log_total, grad_out):
    length = queries.shape[0]
    block_rows = min(512, length)
    scaling = queries.shape[2] ** (-0.5)
    key_index = jnp.arange(length, dtype=jnp.int32)

    def one_block(carry, args):
        grad_keys, grad_values = carry
        query_block, grad_block, total_block, first_row = args
        scores = (
            jnp.einsum("qhd,khd->hqk", query_block, keys_in, preferred_element_type=jnp.float32)
            * scaling
        )
        causal = (first_row + jnp.arange(block_rows, dtype=jnp.int32))[:, None] >= key_index[
            None, :
        ]
        scores = jnp.where(causal[None], scores, -jnp.inf)
        probs = jnp.exp(scores - total_block[..., None])
        grad_probs = jnp.einsum(
            "qhd,khd->hqk", grad_block, values_in, preferred_element_type=jnp.float32
        )
        row_dot = jnp.sum(probs * grad_probs, axis=-1, keepdims=True)
        grad_scores = (probs * (grad_probs - row_dot)).astype(jnp.bfloat16)
        grad_query = (
            jnp.einsum("hqk,khd->qhd", grad_scores, keys_in, preferred_element_type=jnp.float32)
            * scaling
        )
        grad_keys = (
            grad_keys
            + jnp.einsum(
                "hqk,qhd->khd", grad_scores, query_block, preferred_element_type=jnp.float32
            )
            * scaling
        )
        grad_values = grad_values + jnp.einsum(
            "hqk,qhd->khd",
            probs.astype(jnp.bfloat16),
            grad_block,
            preferred_element_type=jnp.float32,
        )
        return ((grad_keys, grad_values), grad_query)

    block_shape = (length // block_rows, block_rows, queries.shape[1], queries.shape[2])
    starts = jnp.arange(length // block_rows, dtype=jnp.int32) * block_rows
    zeros = jnp.zeros(keys_in.shape, jnp.float32)
    (grad_keys, grad_values), grad_queries = lax.scan(
        one_block,
        (zeros, zeros),
        (queries.reshape(block_shape), grad_out.reshape(block_shape), log_total, starts),
    )
    return (grad_queries.reshape(queries.shape), grad_keys, grad_values)


def on_device(
    tokens,
    ln1_gain,
    ln1_bias,
    qkv_weight,
    qkv_bias,
    out_weight,
    ln2_gain,
    ln2_bias,
    gate_up_weight,
    down_weight,
    out_grad,
):
    tok_rows = tokens.shape[1]
    width = tokens.shape[2]
    residual = tokens.reshape(tok_rows, width).astype(jnp.float32)
    cotangent = out_grad.reshape(tok_rows, width)
    qkv_full, proj_full = (
        lax.all_gather(qkv_weight, ("seq", "fsdp"), axis=0, tiled=True),
        lax.all_gather(out_weight, ("seq", "fsdp"), axis=0, tiled=True),
    )
    normed1, ln1_pull = jax.vjp(layer_norm, residual, ln1_gain, ln1_bias)
    hidden1 = normed1.astype(jnp.bfloat16)
    projected = jnp.dot(hidden1, qkv_full, preferred_element_type=jnp.float32) + qkv_bias
    projected = projected.reshape(tok_rows, 3, H, HD)
    positions = lax.axis_index("seq") * tok_rows + jnp.arange(tok_rows, dtype=jnp.int32)
    packed = jnp.stack(
        [rotate(projected[:, 0], positions), rotate(projected[:, 1], positions), projected[:, 2]],
        axis=1,
    )
    packed = packed.reshape(tok_rows, 3, width).astype(jnp.bfloat16)
    by_heads = lax.all_to_all(packed, "seq", split_axis=2, concat_axis=0, tiled=True)
    length = by_heads.shape[0]
    local_heads = by_heads.shape[2] // HD
    queries = by_heads[:, 0].reshape(length, local_heads, HD)
    keys_in = by_heads[:, 1].reshape(length, local_heads, HD)
    values_in = by_heads[:, 2].reshape(length, local_heads, HD)
    attended, log_total = attend(queries, keys_in, values_in)
    attended_b = attended.reshape(length, local_heads * HD).astype(jnp.bfloat16)
    gathered_out = lax.all_to_all(attended_b, "seq", split_axis=0, concat_axis=1, tiled=True)
    middle = residual + jnp.dot(gathered_out, proj_full, preferred_element_type=jnp.float32)
    gate_up_full, down_full = (
        lax.all_gather(gate_up_weight, ("seq", "fsdp"), axis=0, tiled=True),
        lax.all_gather(down_weight, ("seq", "fsdp"), axis=0, tiled=True),
    )
    normed2, ln2_pull = jax.vjp(layer_norm, middle, ln2_gain, ln2_bias)
    hidden2 = normed2.astype(jnp.bfloat16)
    gate_up = jnp.dot(hidden2, gate_up_full, preferred_element_type=jnp.float32)
    activation, swiglu_pull = jax.vjp(swiglu, gate_up)
    activation_b = activation.astype(jnp.bfloat16)
    block_out = (
        middle + jnp.dot(activation_b, down_full, preferred_element_type=jnp.float32)
    ).astype(jnp.bfloat16)
    gate_up_back, down_back = (
        lax.all_gather(gate_up_weight, ("seq", "fsdp"), axis=0, tiled=True),
        lax.all_gather(down_weight, ("seq", "fsdp"), axis=0, tiled=True),
    )
    grad_act = contract_last(cotangent, down_back)
    down_grad = lax.psum_scatter(
        column_term(activation_b, cotangent), ("seq", "fsdp"), scatter_dimension=0, tiled=True
    )
    (grad_gate_up,) = swiglu_pull(grad_act)
    grad_gate_up_b = grad_gate_up.astype(jnp.bfloat16)
    gate_up_grad = lax.psum_scatter(
        column_term(hidden2, grad_gate_up_b), ("seq", "fsdp"), scatter_dimension=0, tiled=True
    )
    grad_hidden2 = contract_last(grad_gate_up_b, gate_up_back)
    grad_middle, ln2_gain_part, ln2_bias_part = ln2_pull(grad_hidden2)
    grad_middle = grad_middle + cotangent.astype(jnp.float32)
    grad_middle_b = grad_middle.astype(jnp.bfloat16)
    qkv_back, proj_back = (
        lax.all_gather(qkv_weight, ("seq", "fsdp"), axis=0, tiled=True),
        lax.all_gather(out_weight, ("seq", "fsdp"), axis=0, tiled=True),
    )
    out_weight_grad = lax.psum_scatter(
        column_term(gathered_out, grad_middle_b), ("seq", "fsdp"), scatter_dimension=0, tiled=True
    )
    grad_out_tok = contract_last(grad_middle_b, proj_back).astype(jnp.bfloat16)
    grad_heads = lax.all_to_all(grad_out_tok, "seq", split_axis=1, concat_axis=0, tiled=True)
    grad_query, grad_key, grad_value = attend_back(
        queries, keys_in, values_in, log_total, grad_heads.reshape(length, local_heads, HD)
    )
    head_positions = jnp.arange(length, dtype=jnp.int32)
    grad_packed = jnp.stack(
        [unrotate(grad_query, head_positions), unrotate(grad_key, head_positions), grad_value],
        axis=1,
    )
    grad_packed = grad_packed.reshape(length, 3, local_heads * HD).astype(jnp.bfloat16)
    grad_tokens = lax.all_to_all(grad_packed, "seq", split_axis=0, concat_axis=2, tiled=True)
    grad_projected = grad_tokens.reshape(tok_rows, 3 * width)
    qkv_weight_grad = lax.psum_scatter(
        column_term(hidden1, grad_projected), ("seq", "fsdp"), scatter_dimension=0, tiled=True
    )
    grad_hidden1 = contract_last(grad_projected, qkv_back)
    bias_part = jnp.sum(grad_projected.astype(jnp.float32), axis=0)
    grad_input, ln1_gain_part, ln1_bias_part = ln1_pull(grad_hidden1)
    grad_input = grad_input + grad_middle
    summed = lax.psum(
        (ln1_gain_part, ln1_bias_part, bias_part, ln2_gain_part, ln2_bias_part), ("seq", "fsdp")
    )
    return (
        block_out.reshape(1, tok_rows, width),
        grad_input.reshape(1, tok_rows, width),
        summed[0],
        summed[1],
        qkv_weight_grad,
        summed[2],
        out_weight_grad,
        summed[3],
        summed[4],
        gate_up_grad,
        down_grad,
    )


def solution(mesh):
    placed = (
        P("fsdp", "seq", None),
        P(),
        P(),
        P(("seq", "fsdp"), None),
        P(),
        P(("seq", "fsdp"), None),
        P(),
        P(),
        P(("seq", "fsdp"), None),
        P(("seq", "fsdp"), None),
        P("fsdp", "seq", None),
    )
    return jax.shard_map(
        on_device,
        mesh=mesh,
        in_specs=placed,
        out_specs=(
            P("fsdp", "seq", None),
            P("fsdp", "seq", None),
            P(),
            P(),
            P(("seq", "fsdp"), None),
            P(),
            P(("seq", "fsdp"), None),
            P(),
            P(),
            P(("seq", "fsdp"), None),
            P(("seq", "fsdp"), None),
        ),
        check_vma=False,
    )
```

profile of v0, /device:TPU:0, one launch (start us, length us, event | category | flops | bytes accessed | tf_op | source)
XLA Modules:
  0.0 1387.9 jit_solution(4007856806318512705)
XLA Ops:
  12.9 70.3 %all-gather.5.cloned.1.call-done = bf16[1024,3072]{1,0:T(8,128)(2,1)} async-done(((bf16[32,3072]{1,0:T(8,128)(2,1)}), bf16[1024,3072]{1,0:T(8,128)(2,1)}) %all-gather.5.cloned.1.call-update) | async-done | bytes 6291472 | tf_op jit(solution)/shard_map/all_gather | solution.py:175
  83.2 3.9 convolution_add_fusion
  88.0 1.7 copy.58
  89.7 3.6 all-to-all-start
  93.3 30.2 %all-to-all-done = bf16[128,3,1024]{0,1,2:T(4,128)(2,1)S(1)} async-done(((bf16[128,3,1024]{0,1,2:T(4,128)(2,1)}), bf16[128,3,1024]{0,1,2:T(4,128)(2,1)S(1)}, u32[]{:S(2)}, u32[]{:S(2)}) %all-to-all-start) | async-done | bytes 786464 | tf_op jit(solution)/shard_map/all_to_all | solution.py:188
  126.1 14.4 %while.28 = (s32[]{:T(128)}, bf16[2,512,2,64]{1,3,2,0:T(8,128)(2,1)S(1)}, f32[2,2,512]{2,1,0:T(2,128)S(1)}, s32[2]{0:T(128)S(1)}, bf16[2,512,2,64]{1,3,2,0:T(8,1...) while((s32[]{:T(128)}, ...), condition=%wide.region_5.6_spmd.clone, body=%wide.region_2.5_spmd.clone.sunk | while | flops 281542144 | bytes 15634553 | solution.py:100
  127.7 2.0 fusion.139
  130.8 2.4 fusion.141
  134.9 2.0 fusion.139
  138.1 2.4 fusion.141
  141.8 3.6 all-to-all-start.1
  145.4 9.4 all-to-all-done.1
  154.9 2.2 fusion.94
  157.3 79.5 %all-gather.9.cloned.1.call-done = bf16[1024,5632]{1,0:T(8,128)(2,1)} async-done(((bf16[32,5632]{1,0:T(8,128)(2,1)}), bf16[1024,5632]{1,0:T(8,128)(2,1)}) %all-gather.9.cloned.1.call-update) | async-done | bytes 11534352 | tf_op jit(solution)/shard_map/all_gather | solution.py:199
  236.8 7.7 fusion.90
  244.5 60.7 %all-gather.11.cloned.1.call-done = bf16[2816,1024]{1,0:T(8,128)(2,1)} async-done(((bf16[88,1024]{1,0:T(8,128)(2,1)}), bf16[2816,1024]{1,0:T(8,128)(2,1)}) %all-gather.11.cloned.1.call-update) | async-done | bytes 5767184 | tf_op jit(solution)/shard_map/all_gather | solution.py:200
  305.2 7.7 fusion.84
  313.0 6.6 multiply_reduce_fusion.1
  319.5 1.3 fusion.92
  322.7 1.5 convolution_convert_fusion
  324.3 1.8 copy.71
  326.1 3.6 all-to-all-start.2
  329.7 3.6 fusion.95
  333.8 5.6 all-to-all-done.2
  340.4 42.1 %while.29 = (s32[]{:T(128)}, f32[1024,2,64]{0,2,1:T(8,128)}, f32[1024,2,64]{0,2,1:T(8,128)}, f32[2,512,2,64]{1,0,3,2:T(2,128)}, bf16[2,512,2,64]{1,3,2,0:T(8,128...) while((s32[]{:T(128)}, f32[1024,2,64]{0,2,1:T(8,128)}, ...), condition=%wide.region_12.13_spmd.clone, body=%wide.region_10.12_spmd.clone.sunk | while | flops 688061952 | bytes 55083208 | solution.py:149
  340.4 1.6 fusion.151
  343.8 2.8 multiply_reduce_fusion.5
  346.6 1.3 multiply_convert_fusion.3
  347.9 2.2 fusion.152
  350.1 4.4 fusion.153
  355.6 5.7 dynamic_update_slice.21
  361.3 1.6 fusion.151
  364.7 2.8 multiply_reduce_fusion.5
  367.5 1.3 multiply_convert_fusion.3
  368.8 2.4 fusion.152
  371.2 4.5 fusion.153
  376.8 5.7 dynamic_update_slice.21
  384.7 1.5 reshape.364
  388.0 33.2 %all_to_all.65 = bf16[1024,3,128]{2,1,0:T(4,128)(2,1)S(1)} all-to-all(bf16[1024,3,128]{2,1,0:T(4,128)(2,1)S(1)} %copy.68), channel_id=1, replica_groups=mesh['seq'=8,'fsdp'=4] {'seq'}, dimensions={0} | all-to-all | bytes 1572864 | tf_op jit(solution)/shard_map/all_to_all | solution.py:245
  421.9 6.5 fusion.67
  429.6 5.9 fusion.70
  436.8 10.9 fusion.82
  448.8 4.3 fusion.48
  453.1 5.1 fusion.91
  458.6 38.4 %all-reduce.2 = (f32[1024]{0:T(1024)}, f32[1024]{0:T(1024)}, f32[3072]{0:T(1024)}, f32[1024]{0:T(1024)}, f32[1024]{0:T(1024)}) all-reduce(f32[1024]{0:T(1024)S(1)} %get-tuple-element.239, f32[1024]{0:T(1024)S(1)} %get-tuple-element.242, f32[3072]{0:T(1024)S(1)} %bitcast.210, ...), channel_id=1, replica_groups=mesh['seq'=8,'fsdp'=4] {'seq','fsdp'}, use_global_device_ids=true, to_apply=%region_16.17 | all-reduce | flops 7168 | bytes 57344 | tf_op jit(solution)/shard_map/psum | solution.py:254
  498.1 138.9 %reduce-scatter.5.cloned.1.call-done = f32[32,3072]{1,0:T(8,128)} async-done(((f32[1024,3072]{1,0:T(8,128)}), f32[32,3072]{1,0:T(8,128)}) %reduce-scatter.5.cloned.1.call-update) | async-done | bytes 393232 | tf_op jit(solution)/shard_map/reduce_scatter | solution.py:247
  637.1 250.8 %reduce-scatter.11.cloned.1.call-done = f32[88,1024]{1,0:T(8,128)} async-done(((f32[2816,1024]{1,0:T(8,128)}), f32[88,1024]{1,0:T(8,128)}) %reduce-scatter.11.cloned.1.call-update) | async-done | bytes 360464 | tf_op jit(solution)/shard_map/reduce_scatter | solution.py:215
  887.9 493.1 %reduce-scatter.9.cloned.1.call-done = f32[32,5632]{1,0:T(8,128)} async-done(((f32[1024,5632]{1,0:T(8,128)}), f32[32,5632]{1,0:T(8,128)}) %reduce-scatter.9.cloned.1.call-update) | async-done | bytes 720912 | tf_op jit(solution)/shard_map/reduce_scatter | solution.py:220
  (134 shorter events, 34.6 us)
Async XLA Ops:
  7.2 76.0 %all-gather.5.cloned.1.call-start = ((), (), s32[]{:S(2)}) async-start(), calls=%async_computation.8 | async-start | bytes 6488064 | tf_op jit(solution)/shard_map/all_gather | solution.py:175
  7.9 137.5 %all-gather.7.cloned.1.call-start = ((), (), s32[]{:S(2)}) async-start(), calls=%async_computation.9 | async-start | bytes 2162688 | tf_op jit(solution)/shard_map/all_gather | solution.py:176
  8.7 228.1 %all-gather.9.cloned.1.call-start = ((), (), s32[]{:S(2)}) async-start(), calls=%async_computation.10 | async-start | bytes 11894784 | tf_op jit(solution)/shard_map/all_gather | solution.py:199
  9.4 295.8 %all-gather.11.cloned.1.call-start = ((), (), s32[]{:S(2)}) async-start(), calls=%async_computation.11 | async-start | bytes 5947392 | tf_op jit(solution)/shard_map/all_gather | solution.py:200
  12.2 0.5 copy-start.17
  89.7 33.8 %all-to-all-start = ((bf16[128,3,1024]{0,1,2:T(4,128)(2,1)}), bf16[128,3,1024]{0,1,2:T(4,128)(2,1)S(1)}, u32[]{:S(2)}, u32[]{:S(2)}) async-start(bf16[128,3,1024]{0,1,2:T(4,128)(2,1)} %copy.58), calls=%async_computation | async-start | bytes 2097152 | tf_op jit(solution)/shard_map/all_to_all | solution.py:188
  126.1 28.7 %copy-start.2 = (bf16[1,128,1024]{2,1,0:T(8,128)(2,1)S(1)}, bf16[1,128,1024]{2,1,0:T(8,128)(2,1)}, u32[]{:S(2)}) copy-start(bf16[1,128,1024]{2,1,0:T(8,128)(2,1)} %param.15) | copy-start | bytes 786436
  140.5 96.3 %copy-start.13 = (f32[1024]{0:T(1024)S(1)}, f32[1024]{0:T(1024)}, u32[]{:S(2)}) copy-start(f32[1024]{0:T(1024)} %param.21) | copy-start | bytes 12292
  140.6 96.3 %copy-start.15 = (f32[1024]{0:T(1024)S(1)}, f32[1024]{0:T(1024)}, u32[]{:S(2)}) copy-start(f32[1024]{0:T(1024)} %param.22) | copy-start | bytes 12292
  141.8 13.1 all-to-all-start.1
  154.8 2.5 copy-start.12
  157.3 147.9 %copy-start.10 = (bf16[1,128,1024]{2,1,0:T(8,128)(2,1)S(1)}, bf16[1,128,1024]{2,1,0:T(8,128)(2,1)}, u32[]{:S(2)}) copy-start(bf16[1,128,1024]{2,1,0:T(8,128)(2,1)} %param.25) | copy-start | bytes 786436
  305.2 7.7 copy-start.1
  313.0 9.8 copy-start.4
  320.8 0.8 copy-start.6
  326.1 13.3 all-to-all-start.2
  329.6 168.5 %reduce-scatter.7.cloned.1.call-start = ((), (), s32[]{:S(2)}) async-start(), calls=%async_computation.13 | async-start | bytes 4325376 | tf_op jit(solution)/shard_map/reduce_scatter | solution.py:231
  333.3 303.8 %reduce-scatter.5.cloned.1.call-start = ((), (), s32[]{:S(2)}) async-start(), calls=%async_computation.12 | async-start | bytes 12976128 | tf_op jit(solution)/shard_map/reduce_scatter | solution.py:247
  342.1 4.5 copy-start
  362.9 4.5 copy-start
  387.2 34.7 %copy-start.3 = (bf16[1,128,1024]{2,1,0:T(8,128)(2,1)S(1)}, bf16[1,128,1024]{2,1,0:T(8,128)(2,1)}, u32[]{:S(2)}) copy-start(bf16[1,128,1024]{2,1,0:T(8,128)(2,1)} %param.15) | copy-start | bytes 786436
  387.2 34.7 %copy-start.14 = (f32[1024]{0:T(1024)S(1)}, f32[1024]{0:T(1024)}, u32[]{:S(2)}) copy-start(f32[1024]{0:T(1024)} %param.16) | copy-start | bytes 12292
  387.2 34.7 %copy-start.16 = (f32[1024]{0:T(1024)S(1)}, f32[1024]{0:T(1024)}, u32[]{:S(2)}) copy-start(f32[1024]{0:T(1024)} %param.17) | copy-start | bytes 12292
  428.4 1.1 copy-start.8
  428.4 1.2 copy-start.11
  428.4 459.5 %reduce-scatter.11.cloned.1.call-start = ((), (), s32[]{:S(2)}) async-start(), calls=%async_computation.15 | async-start | bytes 11894784 | tf_op jit(solution)/shard_map/reduce_scatter | solution.py:215
  435.5 1.4 copy-start.5
  435.5 945.6 %reduce-scatter.9.cloned.1.call-start = ((), (), s32[]{:S(2)}) async-start(), calls=%async_computation.14 | async-start | bytes 23789568 | tf_op jit(solution)/shard_map/reduce_scatter | solution.py:220
  447.7 1.1 copy-start.9
  453.1 5.1 copy-start.18
  453.1 44.0 %copy-start.7 = (f32[128,1024]{1,0:T(8,128)S(1)}, f32[128,1024]{1,0:T(8,128)}, u32[]{:S(2)}) copy-start(f32[128,1024]{1,0:T(8,128)} %copy-done.6) | copy-start | bytes 1572868
Sparse Core Ops, SparseCore 0:
  10.9 72.2 all-gather.4
  86.1 57.7 all-gather.6
  146.7 90.0 all-gather.8
  239.5 65.6 all-gather.10
  333.4 143.9 reduce-scatter.6
  483.9 153.1 reduce-scatter.4
  640.1 247.7 reduce-scatter.10
  890.9 490.1 reduce-scatter.8
where the time goes:
time: 1390 us
  waiting for transfers between devices  1140 us (82%)
  matrix products  98.6 us (7%)
  blocking collectives  71.7 us (5%)
  local copies, waits for them, and re-layouts  31.8 us (2%)
  other arithmetic  18.2 us (1%)
  between operations  14.6 us (1%)
    reduce_scatter x1, waiting for transfers between devices, on_device(): lax.psum_scatter(column_term(hidden2, grad_gate_up_b), ('seq', 'fsdp'), s...  493 us
    reduce_scatter x1, waiting for transfers between devices, on_device(): lax.psum_scatter(column_term(activation_b, cotangent), ('seq', 'fsdp'), s...  251 us
    reduce_scatter x1, waiting for transfers between devices, on_device(): lax.psum_scatter(column_term(hidden1, grad_projected), ('seq', 'fsdp'), s...  139 us
    all_gather x1, waiting for transfers between devices, on_device(): lax.all_gather(gate_up_weight, ('seq', 'fsdp'), axis=0, tiled=True)  79.5 us
    all_gather x1, waiting for transfers between devices, on_device(): lax.all_gather(qkv_weight, ('seq', 'fsdp'), axis=0, tiled=True)  70.3 us
    all_gather x1, waiting for transfers between devices, on_device(): lax.all_gather(down_weight, ('seq', 'fsdp'), axis=0, tiled=True)  60.7 us
    psum x1, blocking collectives, on_device(): lax.psum((ln1_gain_part, ln1_bias_part, bias_part, ln2_gain_part, ln2_bia...  38.4 us
    all_to_all x1, blocking collectives, on_device(): lax.all_to_all(grad_packed, 'seq', split_axis=0, concat_axis=2, tiled=True)  33.2 us
  transfers between devices with their start and end apart: 11, of which 9 were waited for; matrix products, arithmetic and copies ran while one was open for 9% of the time, Pallas kernels for 0%

commit v1 on v0

--- a/solution.py
+++ b/solution.py
@@ -185,7 +185,10 @@
         axis=1,
     )
     packed = packed.reshape(tok_rows, 3, width).astype(jnp.bfloat16)
-    by_heads = lax.all_to_all(packed, "seq", split_axis=2, concat_axis=0, tiled=True)
+    by_heads = jnp.concatenate(
+        lax.all_to_all(jnp.stack(jnp.split(packed, lax.axis_size("seq"), axis=2)), "seq", 0, 0),
+        axis=0,
+    )
     length = by_heads.shape[0]
     local_heads = by_heads.shape[2] // HD
     queries = by_heads[:, 0].reshape(length, local_heads, HD)

time: 1390 us -> 1390 us (level)
  transfers between devices with their start and end apart: 11 -> 11, of which waited for: 9 -> 10; matrix products, arithmetic and copies ran while one was open for 9% -> 9% of each run, Pallas kernels for 0% -> 0%
where the time goes in v1:
time: 1390 us
  waiting for transfers between devices  1140 us (82%)
  matrix products  98.7 us (7%)
  blocking collectives  71.7 us (5%)
  local copies, waits for them, and re-layouts  35.2 us (3%)
  other arithmetic  18.2 us (1%)
  between operations  14.6 us (1%)
    reduce_scatter x1, waiting for transfers between devices, on_device(): lax.psum_scatter(column_term(hidden2, grad_gate_up_b), ('seq', 'fsdp'), s...  493 us
    reduce_scatter x1, waiting for transfers between devices, on_device(): lax.psum_scatter(column_term(activation_b, cotangent), ('seq', 'fsdp'), s...  251 us
    reduce_scatter x1, waiting for transfers between devices, on_device(): lax.psum_scatter(column_term(hidden1, grad_projected), ('seq', 'fsdp'), s...  139 us
    all_gather x1, waiting for transfers between devices, on_device(): lax.all_gather(gate_up_weight, ('seq', 'fsdp'), axis=0, tiled=True)  81.1 us
    all_gather x1, waiting for transfers between devices, on_device(): lax.all_gather(qkv_weight, ('seq', 'fsdp'), axis=0, tiled=True)  70.4 us
    all_gather x1, waiting for transfers between devices, on_device(): lax.all_gather(down_weight, ('seq', 'fsdp'), axis=0, tiled=True)  60.7 us
    psum x1, blocking collectives, on_device(): lax.psum((ln1_gain_part, ln1_bias_part, bias_part, ln2_gain_part, ln2_bia...  38.5 us
    all_to_all x1, blocking collectives, on_device(): lax.all_to_all(grad_packed, 'seq', split_axis=0, concat_axis=2, tiled=True)  33.2 us
  transfers between devices with their start and end apart: 11, of which 10 were waited for; matrix products, arithmetic and copies ran while one was open for 9% of the time, Pallas kernels for 0%

profile of v1, /device:TPU:0, one launch (start us, length us, event | category | flops | bytes accessed | tf_op | source)
XLA Modules:
  0.0 1386.7 jit_solution(16244670282660402855)
XLA Ops:
  11.1 1.2 fusion.59
  12.9 70.4 %all-gather.5.cloned.1.call-done = bf16[1024,3072]{1,0:T(8,128)(2,1)} async-done(((bf16[32,3072]{1,0:T(8,128)(2,1)}), bf16[1024,3072]{1,0:T(8,128)(2,1)}) %all-gather.5.cloned.1.call-update) | async-done | bytes 6291472 | tf_op jit(solution)/shard_map/all_gather | solution.py:175
  83.2 3.9 convolution_add_fusion
  93.1 3.5 all-to-all-start
  96.7 23.6 %all-to-all-done = bf16[8,128,3,128]{1,3,2,0:T(8,128)(2,1)S(1)} async-done(((bf16[8,128,3,128]{1,3,2,0:T(8,128)(2,1)}), bf16[8,128,3,128]{1,3,2,0:T(8,128)(2,1)S(1)}, u32[]{:S(2)}, u32[]{:S(2)}) %all-to-all-start) | async-done | bytes 786464 | tf_op jit(solution)/shard_map/all_to_all | solution.py:189
  123.0 14.4 %while.28 = (s32[]{:T(128)}, bf16[2,512,2,64]{1,3,2,0:T(8,128)(2,1)S(1)}, f32[2,2,512]{2,1,0:T(2,128)S(1)}, s32[2]{0:T(128)S(1)}, bf16[2,512,2,64]{1,3,2,0:T(8,1...) while((s32[]{:T(128)}, ...), condition=%wide.region_5.6_spmd.clone, body=%wide.region_2.5_spmd.clone.sunk | while | flops 281542144 | bytes 15634553 | solution.py:100
  124.6 2.0 fusion.147
  127.8 2.4 fusion.149
  131.9 2.0 fusion.147
  135.0 2.4 fusion.149
  138.7 3.6 all-to-all-start.1
  142.4 9.4 all-to-all-done.1
  151.8 2.3 fusion.102
  154.4 81.1 %all-gather.9.cloned.1.call-done = bf16[1024,5632]{1,0:T(8,128)(2,1)} async-done(((bf16[32,5632]{1,0:T(8,128)(2,1)}), bf16[1024,5632]{1,0:T(8,128)(2,1)}) %all-gather.9.cloned.1.call-update) | async-done | bytes 11534352 | tf_op jit(solution)/shard_map/all_gather | solution.py:202
  235.5 7.7 fusion.98
  243.2 60.7 %all-gather.11.cloned.1.call-done = bf16[2816,1024]{1,0:T(8,128)(2,1)} async-done(((bf16[88,1024]{1,0:T(8,128)(2,1)}), bf16[2816,1024]{1,0:T(8,128)(2,1)}) %all-gather.11.cloned.1.call-update) | async-done | bytes 5767184 | tf_op jit(solution)/shard_map/all_gather | solution.py:203
  303.9 7.7 fusion.84
  311.6 6.6 multiply_reduce_fusion.1
  318.2 1.3 fusion.100
  321.4 1.5 convolution_convert_fusion
  323.0 1.8 copy.80
  324.7 3.6 all-to-all-start.2
  328.4 3.6 fusion.103
  332.5 5.6 all-to-all-done.2
  339.1 42.1 %while.29 = (s32[]{:T(128)}, f32[1024,2,64]{0,2,1:T(8,128)}, f32[1024,2,64]{0,2,1:T(8,128)}, f32[2,512,2,64]{1,0,3,2:T(2,128)}, bf16[2,512,2,64]{1,3,2,0:T(8,128...) while((s32[]{:T(128)}, f32[1024,2,64]{0,2,1:T(8,128)}, ...), condition=%wide.region_12.13_spmd.clone, body=%wide.region_10.12_spmd.clone.sunk | while | flops 688061952 | bytes 55083208 | solution.py:149
  339.1 1.6 fusion.159
  342.5 2.8 multiply_reduce_fusion.5
  345.3 1.3 multiply_convert_fusion.3
  346.6 2.2 fusion.160
  348.8 4.4 fusion.161
  354.2 5.7 dynamic_update_slice.21
  360.0 1.6 fusion.159
  363.4 2.8 multiply_reduce_fusion.5
  366.2 1.3 multiply_convert_fusion.3
  367.5 2.4 fusion.160
  369.9 4.5 fusion.161
  375.5 5.7 dynamic_update_slice.21
  383.3 1.5 reshape.368
  386.7 33.2 %all_to_all.52 = bf16[1024,3,128]{2,1,0:T(4,128)(2,1)S(1)} all-to-all(bf16[1024,3,128]{2,1,0:T(4,128)(2,1)S(1)} %copy.77), channel_id=1, replica_groups=mesh['seq'=8,'fsdp'=4] {'seq'}, dimensions={0} | all-to-all | bytes 1572864 | tf_op jit(solution)/shard_map/all_to_all | solution.py:248
  420.6 6.5 fusion.67
  428.2 5.9 fusion.70
  435.5 10.9 fusion.82
  447.5 4.3 fusion.48
  451.8 5.1 fusion.99
  457.3 38.5 %all-reduce.2 = (f32[1024]{0:T(1024)}, f32[1024]{0:T(1024)}, f32[3072]{0:T(1024)}, f32[1024]{0:T(1024)}, f32[1024]{0:T(1024)}) all-reduce(f32[1024]{0:T(1024)S(1)} %get-tuple-element.239, f32[1024]{0:T(1024)S(1)} %get-tuple-element.242, f32[3072]{0:T(1024)S(1)} %bitcast.236, ...), channel_id=1, replica_groups=mesh['seq'=8,'fsdp'=4] {'seq','fsdp'}, use_global_device_ids=true, to_apply=%region_16.17 | all-reduce | flops 7168 | bytes 57344 | tf_op jit(solution)/shard_map/psum | solution.py:257
  496.9 139.1 %reduce-scatter.5.cloned.1.call-done = f32[32,3072]{1,0:T(8,128)} async-done(((f32[1024,3072]{1,0:T(8,128)}), f32[32,3072]{1,0:T(8,128)}) %reduce-scatter.5.cloned.1.call-update) | async-done | bytes 393232 | tf_op jit(solution)/shard_map/reduce_scatter | solution.py:250
  636.0 250.8 %reduce-scatter.11.cloned.1.call-done = f32[88,1024]{1,0:T(8,128)} async-done(((f32[2816,1024]{1,0:T(8,128)}), f32[88,1024]{1,0:T(8,128)}) %reduce-scatter.11.cloned.1.call-update) | async-done | bytes 360464 | tf_op jit(solution)/shard_map/reduce_scatter | solution.py:218
  886.8 493.0 %reduce-scatter.9.cloned.1.call-done = f32[32,5632]{1,0:T(8,128)} async-done(((f32[1024,5632]{1,0:T(8,128)}), f32[32,5632]{1,0:T(8,128)}) %reduce-scatter.9.cloned.1.call-update) | async-done | bytes 720912 | tf_op jit(solution)/shard_map/reduce_scatter | solution.py:223
  (142 shorter events, 38.6 us)
Async XLA Ops:
  7.2 76.0 %all-gather.5.cloned.1.call-start = ((), (), s32[]{:S(2)}) async-start(), calls=%async_computation.8 | async-start | bytes 6488064 | tf_op jit(solution)/shard_map/all_gather | solution.py:175
  7.9 134.5 %all-gather.7.cloned.1.call-start = ((), (), s32[]{:S(2)}) async-start(), calls=%async_computation.9 | async-start | bytes 2162688 | tf_op jit(solution)/shard_map/all_gather | solution.py:176
  8.7 226.8 %all-gather.9.cloned.1.call-start = ((), (), s32[]{:S(2)}) async-start(), calls=%async_computation.10 | async-start | bytes 11894784 | tf_op jit(solution)/shard_map/all_gather | solution.py:202
  9.4 294.5 %all-gather.11.cloned.1.call-start = ((), (), s32[]{:S(2)}) async-start(), calls=%async_computation.11 | async-start | bytes 5947392 | tf_op jit(solution)/shard_map/all_gather | solution.py:203
  12.2 0.5 copy-start.17
  93.1 27.2 %all-to-all-start = ((bf16[8,128,3,128]{1,3,2,0:T(8,128)(2,1)}), bf16[8,128,3,128]{1,3,2,0:T(8,128)(2,1)S(1)}, u32[]{:S(2)}, u32[]{:S(2)}) async-start(bf16[8,128,3,128]{1,3,2,0:T(8,128)(2,1)} %fusion.85), calls=%async_computation | async-start | bytes 1572864 | tf_op jit(solution)/shard_map/all_to_all | solution.py:189
  123.0 28.7 %copy-start.2 = (bf16[1,128,1024]{2,1,0:T(8,128)(2,1)S(1)}, bf16[1,128,1024]{2,1,0:T(8,128)(2,1)}, u32[]{:S(2)}) copy-start(bf16[1,128,1024]{2,1,0:T(8,128)(2,1)} %param.15) | copy-start | bytes 786436
  137.5 98.0 %copy-start.13 = (f32[1024]{0:T(1024)S(1)}, f32[1024]{0:T(1024)}, u32[]{:S(2)}) copy-start(f32[1024]{0:T(1024)} %param.21) | copy-start | bytes 12292
  137.5 98.0 %copy-start.15 = (f32[1024]{0:T(1024)S(1)}, f32[1024]{0:T(1024)}, u32[]{:S(2)}) copy-start(f32[1024]{0:T(1024)} %param.22) | copy-start | bytes 12292
  138.7 13.1 all-to-all-start.1
  151.8 2.6 copy-start.12
  154.4 149.6 %copy-start.10 = (bf16[1,128,1024]{2,1,0:T(8,128)(2,1)S(1)}, bf16[1,128,1024]{2,1,0:T(8,128)(2,1)}, u32[]{:S(2)}) copy-start(bf16[1,128,1024]{2,1,0:T(8,128)(2,1)} %param.25) | copy-start | bytes 786436
  303.9 7.7 copy-start.1
  311.6 9.8 copy-start.4
  319.5 0.8 copy-start.6
  324.7 13.3 all-to-all-start.2
  328.3 168.6 %reduce-scatter.7.cloned.1.call-start = ((), (), s32[]{:S(2)}) async-start(), calls=%async_computation.13 | async-start | bytes 4325376 | tf_op jit(solution)/shard_map/reduce_scatter | solution.py:234
  332.0 304.0 %reduce-scatter.5.cloned.1.call-start = ((), (), s32[]{:S(2)}) async-start(), calls=%async_computation.12 | async-start | bytes 12976128 | tf_op jit(solution)/shard_map/reduce_scatter | solution.py:250
  340.7 4.5 copy-start
  361.6 4.5 copy-start
  385.8 34.7 %copy-start.3 = (bf16[1,128,1024]{2,1,0:T(8,128)(2,1)S(1)}, bf16[1,128,1024]{2,1,0:T(8,128)(2,1)}, u32[]{:S(2)}) copy-start(bf16[1,128,1024]{2,1,0:T(8,128)(2,1)} %param.15) | copy-start | bytes 786436
  385.9 34.7 %copy-start.14 = (f32[1024]{0:T(1024)S(1)}, f32[1024]{0:T(1024)}, u32[]{:S(2)}) copy-start(f32[1024]{0:T(1024)} %param.16) | copy-start | bytes 12292
  385.9 34.7 %copy-start.16 = (f32[1024]{0:T(1024)S(1)}, f32[1024]{0:T(1024)}, u32[]{:S(2)}) copy-start(f32[1024]{0:T(1024)} %param.17) | copy-start | bytes 12292
  427.1 1.1 copy-start.8
  427.1 1.2 copy-start.11
  427.1 459.7 %reduce-scatter.11.cloned.1.call-start = ((), (), s32[]{:S(2)}) async-start(), calls=%async_computation.15 | async-start | bytes 11894784 | tf_op jit(solution)/shard_map/reduce_scatter | solution.py:218
  434.1 1.4 copy-start.5
  434.2 945.7 %reduce-scatter.9.cloned.1.call-start = ((), (), s32[]{:S(2)}) async-start(), calls=%async_computation.14 | async-start | bytes 23789568 | tf_op jit(solution)/shard_map/reduce_scatter | solution.py:223
  446.4 1.1 copy-start.9
  451.8 5.1 copy-start.18
  451.8 44.0 %copy-start.7 = (f32[128,1024]{1,0:T(8,128)S(1)}, f32[128,1024]{1,0:T(8,128)}, u32[]{:S(2)}) copy-start(f32[128,1024]{1,0:T(8,128)} %copy-done.6) | copy-start | bytes 1572868
Sparse Core Ops, SparseCore 0:
  10.9 72.2 all-gather.4
  86.1 56.2 all-gather.6
  145.3 90.1 all-gather.8
  238.2 65.6 all-gather.10
  332.1 143.7 reduce-scatter.6
  482.4 153.5 reduce-scatter.4
  639.0 247.7 reduce-scatter.10
  889.8 490.0 reduce-scatter.8
